TPU v7x, 512 devices: a whole 4x4x16 slice. The times are simulated.
512 devices in a mesh: gx: 16 (over z), gz: 32 (over x, y, core).
Axes of the slice: x: 4, y: 4, z: 16, core: 2. Of those that a mesh axis runs over, the one named last changes fastest.
Arguments:
- velocity: float32 [3, 4096, 1, 4096], P(None, 'gx', None, 'gz'), may hold values from -6 to 6
Outputs:
- advection: float32 [3, 4096, 1, 4096], P(None, 'gx', None, 'gz')
All inputs are finite; a program needn't handle non-finite values.
Results may differ from a plain program's by a relative error of at most 0.00013.
Values sent between devices are 32-bit elements; how exact they have to be, the bound alone decides.
A program may use at most 64 MiB of HBM per device.

v0:
```python
import jax
import jax.numpy as jnp
from jax import lax
from jax.sharding import PartitionSpec as P

ALPHA_D = 1.0 / 3.0
COEF_A = 14.0 / 9.0
COEF_B = 1.0 / 9.0
ALPHA_F = 0.49
block_len = 128


def with_halo(block, sides, width):
    for axis, dim in sides:
        count = lax.axis_size(axis)
        forward = [(i, i + 1) for i in range(count - 1)]
        forward.append((count - 1, 0))
        backward = [(target, source) for source, target in forward]
        low = lax.ppermute(
            lax.slice_in_dim(block, block.shape[dim] - width, None, axis=dim), axis, forward
        )
        high = lax.ppermute(lax.slice_in_dim(block, 0, width, axis=dim), axis, backward)
        block = jnp.concatenate([low, block, high], axis=dim)
    return block


def filter_coefficients():
    return (
        (11.0 + 10.0 * ALPHA_F) / 16.0,
        (15.0 + 34.0 * ALPHA_F) / 32.0,
        (-3.0 + 6.0 * ALPHA_F) / 16.0,
        (1.0 - 2.0 * ALPHA_F) / 32.0,
    )


def tables(length, alpha):
    lower_diag = jnp.concatenate(
        [jnp.zeros((1,), jnp.float32), jnp.full((length - 1,), alpha, jnp.float32)]
    )
    upper_diag = jnp.concatenate(
        [jnp.full((length - 1,), alpha, jnp.float32), jnp.zeros((1,), jnp.float32)]
    )
    main_diag = jnp.ones((length,), jnp.float32)
    identity = jnp.eye(length, dtype=jnp.float32)
    inverse = lax.linalg.tridiagonal_solve(lower_diag, main_diag, upper_diag, identity)
    left_col = alpha * inverse[:, 0]
    right_col = alpha * inverse[:, length - 1]
    coupling = alpha * inverse[0, 0]
    return (inverse, left_col, right_col, coupling)


def offset_slice(extended, offset, length, direction, base=3):
    return lax.slice_in_dim(extended, base + offset, base + offset + length, axis=direction)


def slope_rhs(extended, length, direction, base=3):
    rhs = (
        COEF_A
        * 0.5
        * (
            offset_slice(extended, 1, length, direction, base)
            - offset_slice(extended, -1, length, direction, base)
        )
    )
    return rhs + COEF_B * 0.25 * (
        offset_slice(extended, 2, length, direction, base)
        - offset_slice(extended, -2, length, direction, base)
    )


def smooth_rhs(extended, length, direction, base=3):
    coefficients = filter_coefficients()
    rhs = coefficients[0] * offset_slice(extended, 0, length, direction, base)
    for offset in range(1, 4):
        rhs = rhs + 0.5 * coefficients[offset] * (
            offset_slice(extended, offset, length, direction, base)
            + offset_slice(extended, -offset, length, direction, base)
        )
    return rhs


def wrap_pad(values, direction):
    length = values.shape[direction]
    return jnp.concatenate(
        [
            lax.slice_in_dim(values, length - 3, length, axis=direction),
            values,
            lax.slice_in_dim(values, 0, 3, axis=direction),
        ],
        axis=direction,
    )


def apply_along(inverse, values, direction):
    rotated = jnp.tensordot(
        inverse, values, axes=([1], [direction]), precision=lax.Precision.HIGHEST
    )
    return jnp.moveaxis(rotated, 0, direction)


def end_values(partial_value, direction):
    length = partial_value.shape[direction]
    first_val = lax.slice_in_dim(partial_value, 0, 1, axis=direction)
    last_val = lax.slice_in_dim(partial_value, length - 1, length, axis=direction)
    return (first_val, last_val)


def corrected(partial_value, prev_last, next_first, table, direction):
    inverse, left_col, right_col, coupling = table
    first_val, last_val = end_values(partial_value, direction)
    factor_inv = 1.0 / (1.0 - coupling * coupling)
    left_value = (prev_last - coupling * first_val) * factor_inv
    right_value = (next_first - coupling * last_val) * factor_inv
    dims_list = [1] * partial_value.ndim
    dims_list[direction] = partial_value.shape[direction]
    return (
        partial_value
        - left_col.reshape(dims_list) * left_value
        - right_col.reshape(dims_list) * right_value
    )


def extend_x(values):
    return with_halo(values, (("gx", 1),), 3)


def solve_x(rhs, table):
    partial_value = apply_along(table[0], rhs, 1)
    first_val, last_val = end_values(partial_value, 1)
    beside = with_halo(jnp.concatenate([first_val, last_val], axis=1), (("gx", 1),), 1)
    return corrected(partial_value, beside[:, 0:1], beside[:, 3:4], table, 1)


def solve_blocks(rhs, table):
    dims_list = rhs.shape
    blocks = rhs.reshape(dims_list[:-1] + (dims_list[-1] // block_len, block_len))
    last_dim = blocks.ndim - 1
    partial_value = apply_along(table[0], blocks, last_dim)
    first_val, last_val = end_values(partial_value, last_dim)
    prev_last = jnp.roll(last_val, 1, axis=last_dim - 1)
    next_first = jnp.roll(first_val, -1, axis=last_dim - 1)
    return corrected(partial_value, prev_last, next_first, table, last_dim).reshape(dims_list)


def z_part(velocity):
    slope_z = tables(block_len, ALPHA_D)
    pencil = lax.all_to_all(velocity, "gz", split_axis=1, concat_axis=3, tiled=True)
    along_z = pencil[2:3]
    fields = jnp.concatenate([pencil, along_z * pencil], axis=0)
    slopes = solve_blocks(slope_rhs(wrap_pad(fields, 3), fields.shape[3], 3), slope_z)
    local_terms = slopes[3:] + along_z * slopes[:3]
    return lax.all_to_all(local_terms, "gz", split_axis=3, concat_axis=1, tiled=True)


def per_device(velocity):
    width_x = velocity.shape[1]
    slope_x = tables(width_x, ALPHA_D)
    smooth_x = tables(width_x, ALPHA_F)
    along_x = velocity[0:1]
    rim_source = jnp.concatenate([velocity, along_x * velocity], axis=0)
    padded = extend_x(rim_source)
    slopes_x = solve_x(slope_rhs(padded, width_x, 1), slope_x)
    x_terms = slopes_x[3:] + along_x * slopes_x[:3]
    z_terms = z_part(velocity)
    combined = 0.5 * (x_terms + z_terms)
    smoothed = solve_x(smooth_rhs(extend_x(combined), width_x, 1), smooth_x)
    return -smoothed


def solution(mesh):
    return jax.shard_map(
        per_device,
        mesh=mesh,
        in_specs=(P(None, "gx", None, "gz"),),
        out_specs=P(None, "gx", None, "gz"),
        check_vma=False,
    )
```

profile of v0, /device:TPU:2, one launch (start us, length us, event | category | flops | bytes accessed | tf_op | source)
XLA Modules:
  0.0 653.2 jit_solution(18233440407456017549)
XLA Ops:
  2.0 9.5 %all-to-all-start = ((f32[3,256,1,128]{3,2,0,1:T(1,128)}), f32[3,256,1,128]{3,2,0,1:T(1,128)S(1)}, u32[]{:S(2)}, u32[]{:S(2)}) async-start(f32[3,256,1,128]{3,2,0,1:T(1,128)} %copy.113), calls=%async_computation | async-start | bytes 786432 | tf_op jit(solution)/shard_map/all_to_all | solution.py:147
  14.8 9.6 %collective-permute-start = (f32[6,3,1,128]{3,1,0,2:T(4,128)S(1)}, f32[6,3,1,128]{3,1,0,2:T(4,128)S(1)}, u32[]{:S(2)}, u32[]{:S(2)}) collective-permute-start(f32[6,3,1,128]{3,1,0,2:T(4,128)S(1)} %get-tuple-element.1127), channel_id=1, source_target_pairs={{32,0},{64,32},{96,64},{128,96},{160,128},{192,160},{224,192},{256... | collective-permute-start | bytes 27656 | tf_op jit(solution)/shard_map/ppermute | solution.py:22
  26.4 5.8 while.100
  33.8 14.9 %while.98 = (s32[]{:T(128)}, f32[]{:T(128)}, f32[256]{0:T(256)S(1)}, f32[7,32]{1,0:T(8,128)S(1)}, f32[7,32,256]{2,1,0:T(8,128)S(1)}, /*index=5*/f32[7,32,256]{2,...) while((s32[]{:T(128)}, f32[]{:T(128)}, ...), condition=%wide.region_5.6_spmd, body=%wide.region_4.5_spmd.sunk | while | flops 24705 | bytes 267885 | solution.py:45
  50.4 14.9 %while.96 = (s32[]{:T(128)}, f32[]{:T(128)}, f32[256]{0:T(256)S(1)}, f32[7,32]{1,0:T(8,128)S(1)}, f32[7,32,256]{2,1,0:T(8,128)S(1)}, /*index=5*/f32[7,32,256]{2,...) while((s32[]{:T(128)}, f32[]{:T(128)}, ...), condition=%wide.region_1.2_spmd, body=%wide.region_0.1_spmd.sunk | while | flops 24705 | bytes 267885 | solution.py:45
  68.5 64.5 %while.101 = (s32[]{:T(128)}, f32[128]{0:T(128)S(1)}, f32[3,32,128]{2,1,0:T(8,128)S(1)}, f32[3,32,128]{2,1,0:T(8,128)S(1)}, f32[3,32]{1,0:T(4,128)S(1)}, /*index...) while((s32[]{:T(128)}, f32[128]{0:T(128)S(1)}, ...), condition=%wide.region_11.12_spmd, body=%wide.region_10.11_spmd.sunk | while | flops 8226 | bytes 101341 | solution.py:45
  69.9 19.9 %fusion.491 = (f32[128]{0:T(128)S(1)}, f32[128]{0:T(128)S(1)}, f32[128]{0:T(128)S(1)}, f32[128]{0:T(128)S(1)}, f32[128]{0:T(128)S(1)}, /*index=5*/f32[128]{0:T(1...) fusion(f32[3,32,128]{2,1,0:T(8,128)S(1)} %get-tuple-element.256, ...), kind=kLoop, calls=%fused_computation.428.clone.1 | loop fusion | flops 8192 | bytes 33536 | tf_op jit(solution)/shard_map/while/body/eval_jaxpr/sub | solution.py:45
  91.4 19.9 %fusion.491 = (f32[128]{0:T(128)S(1)}, f32[128]{0:T(128)S(1)}, f32[128]{0:T(128)S(1)}, f32[128]{0:T(128)S(1)}, f32[128]{0:T(128)S(1)}, /*index=5*/f32[128]{0:T(1...) fusion(f32[3,32,128]{2,1,0:T(8,128)S(1)} %get-tuple-element.256, ...), kind=kLoop, calls=%fused_computation.428.clone.1 | loop fusion | flops 8192 | bytes 33536 | tf_op jit(solution)/shard_map/while/body/eval_jaxpr/sub | solution.py:45
  112.9 19.9 %fusion.491 = (f32[128]{0:T(128)S(1)}, f32[128]{0:T(128)S(1)}, f32[128]{0:T(128)S(1)}, f32[128]{0:T(128)S(1)}, f32[128]{0:T(128)S(1)}, /*index=5*/f32[128]{0:T(1...) fusion(f32[3,32,128]{2,1,0:T(8,128)S(1)} %get-tuple-element.256, ...), kind=kLoop, calls=%fused_computation.428.clone.1 | loop fusion | flops 8192 | bytes 33536 | tf_op jit(solution)/shard_map/while/body/eval_jaxpr/sub | solution.py:45
  134.1 2.7 fusion.343
  136.8 2.7 fusion.342
  139.6 2.6 fusion.341
  144.8 2.7 fusion.339
  150.1 2.7 fusion.337
  152.7 2.9 fusion.336
  155.6 2.7 fusion.335
  158.3 2.7 fusion.334
  161.0 2.7 fusion.333
  166.3 2.6 fusion.331
  168.9 2.6 fusion.330
  175.7 153.7 %while.99 = (s32[]{:T(128)}, f32[256]{0:T(256)S(1)}, f32[7,32,256]{2,1,0:T(8,128)S(1)}, f32[7,32,256]{2,1,0:T(8,128)S(1)}, f32[7,32]{1,0:T(8,128)S(1)}, /*index=...) while((s32[]{:T(128)}, f32[256]{0:T(256)S(1)}, ...), condition=%wide.region_7.8_spmd, body=%wide.region_6.7_spmd.sunk | while | flops 16418 | bytes 266721 | solution.py:45
  177.4 20.2 %multiply_subtract_fusion.253 = (f32[256]{0:T(256)S(1)}, f32[256]{0:T(256)S(1)}, f32[256]{0:T(256)S(1)}, f32[256]{0:T(256)S(1)}, f32[256]{0:T(256)S(1)}, /*index...) fusion(f32[256]{0:T(256)S(1)} %bitcast.3158, ...), kind=kLoop, calls=%fused_computation.230.clone.1 | loop fusion | flops 16384 | bytes 66688 | tf_op jit(solution)/shard_map/while/body/eval_jaxpr/sub | solution.py:45
  199.4 20.2 %multiply_subtract_fusion.253 = (f32[256]{0:T(256)S(1)}, f32[256]{0:T(256)S(1)}, f32[256]{0:T(256)S(1)}, f32[256]{0:T(256)S(1)}, f32[256]{0:T(256)S(1)}, /*index...) fusion(f32[256]{0:T(256)S(1)} %bitcast.3158, ...), kind=kLoop, calls=%fused_computation.230.clone.1 | loop fusion | flops 16384 | bytes 66688 | tf_op jit(solution)/shard_map/while/body/eval_jaxpr/sub | solution.py:45
  221.3 20.2 %multiply_subtract_fusion.253 = (f32[256]{0:T(256)S(1)}, f32[256]{0:T(256)S(1)}, f32[256]{0:T(256)S(1)}, f32[256]{0:T(256)S(1)}, f32[256]{0:T(256)S(1)}, /*index...) fusion(f32[256]{0:T(256)S(1)} %bitcast.3158, ...), kind=kLoop, calls=%fused_computation.230.clone.1 | loop fusion | flops 16384 | bytes 66688 | tf_op jit(solution)/shard_map/while/body/eval_jaxpr/sub | solution.py:45
  243.3 20.2 %multiply_subtract_fusion.253 = (f32[256]{0:T(256)S(1)}, f32[256]{0:T(256)S(1)}, f32[256]{0:T(256)S(1)}, f32[256]{0:T(256)S(1)}, f32[256]{0:T(256)S(1)}, /*index...) fusion(f32[256]{0:T(256)S(1)} %bitcast.3158, ...), kind=kLoop, calls=%fused_computation.230.clone.1 | loop fusion | flops 16384 | bytes 66688 | tf_op jit(solution)/shard_map/while/body/eval_jaxpr/sub | solution.py:45
  265.2 20.2 %multiply_subtract_fusion.253 = (f32[256]{0:T(256)S(1)}, f32[256]{0:T(256)S(1)}, f32[256]{0:T(256)S(1)}, f32[256]{0:T(256)S(1)}, f32[256]{0:T(256)S(1)}, /*index...) fusion(f32[256]{0:T(256)S(1)} %bitcast.3158, ...), kind=kLoop, calls=%fused_computation.230.clone.1 | loop fusion | flops 16384 | bytes 66688 | tf_op jit(solution)/shard_map/while/body/eval_jaxpr/sub | solution.py:45
  287.2 20.2 %multiply_subtract_fusion.253 = (f32[256]{0:T(256)S(1)}, f32[256]{0:T(256)S(1)}, f32[256]{0:T(256)S(1)}, f32[256]{0:T(256)S(1)}, f32[256]{0:T(256)S(1)}, /*index...) fusion(f32[256]{0:T(256)S(1)} %bitcast.3158, ...), kind=kLoop, calls=%fused_computation.230.clone.1 | loop fusion | flops 16384 | bytes 66688 | tf_op jit(solution)/shard_map/while/body/eval_jaxpr/sub | solution.py:45
  309.2 20.2 %multiply_subtract_fusion.253 = (f32[256]{0:T(256)S(1)}, f32[256]{0:T(256)S(1)}, f32[256]{0:T(256)S(1)}, f32[256]{0:T(256)S(1)}, f32[256]{0:T(256)S(1)}, /*index...) fusion(f32[256]{0:T(256)S(1)} %bitcast.3158, ...), kind=kLoop, calls=%fused_computation.230.clone.1 | loop fusion | flops 16384 | bytes 66688 | tf_op jit(solution)/shard_map/while/body/eval_jaxpr/sub | solution.py:45
  329.4 19.3 %multiply_subtract_fusion.66 = (f32[256]{0:T(256)S(1)}, f32[256]{0:T(256)S(1)}, f32[256]{0:T(256)S(1)}, f32[256]{0:T(256)S(1)}, f32[256]{0:T(256)S(1)}, /*index=...) fusion(f32[256]{0:T(256)S(1)} %bitcast.3585, ...), kind=kLoop, calls=%fused_computation.598 | loop fusion | flops 15872 | bytes 64636 | tf_op jit(solution)/shard_map/eval_jaxpr/sub | solution.py:45
  351.1 152.3 %while.97 = (s32[]{:T(128)}, f32[256]{0:T(256)S(1)}, f32[7,32,256]{2,1,0:T(8,128)S(1)}, f32[7,32,256]{2,1,0:T(8,128)S(1)}, f32[7,32]{1,0:T(8,128)S(1)}, /*index=...) while((s32[]{:T(128)}, f32[256]{0:T(256)S(1)}, ...), condition=%wide.region_3.4_spmd, body=%wide.region_2.3_spmd.sunk | while | flops 16418 | bytes 266721 | solution.py:45
  352.8 20.0 %multiply_subtract_fusion.252 = (f32[256]{0:T(256)S(1)}, f32[256]{0:T(256)S(1)}, f32[256]{0:T(256)S(1)}, f32[256]{0:T(256)S(1)}, f32[256]{0:T(256)S(1)}, /*index...) fusion(f32[256]{0:T(256)S(1)} %bitcast.3176, ...), kind=kLoop, calls=%fused_computation.99.clone.1 | loop fusion | flops 16384 | bytes 66688 | tf_op jit(solution)/shard_map/while/body/eval_jaxpr/sub | solution.py:45
  374.5 20.0 %multiply_subtract_fusion.252 = (f32[256]{0:T(256)S(1)}, f32[256]{0:T(256)S(1)}, f32[256]{0:T(256)S(1)}, f32[256]{0:T(256)S(1)}, f32[256]{0:T(256)S(1)}, /*index...) fusion(f32[256]{0:T(256)S(1)} %bitcast.3176, ...), kind=kLoop, calls=%fused_computation.99.clone.1 | loop fusion | flops 16384 | bytes 66688 | tf_op jit(solution)/shard_map/while/body/eval_jaxpr/sub | solution.py:45
  396.3 20.0 %multiply_subtract_fusion.252 = (f32[256]{0:T(256)S(1)}, f32[256]{0:T(256)S(1)}, f32[256]{0:T(256)S(1)}, f32[256]{0:T(256)S(1)}, f32[256]{0:T(256)S(1)}, /*index...) fusion(f32[256]{0:T(256)S(1)} %bitcast.3176, ...), kind=kLoop, calls=%fused_computation.99.clone.1 | loop fusion | flops 16384 | bytes 66688 | tf_op jit(solution)/shard_map/while/body/eval_jaxpr/sub | solution.py:45
  418.0 20.0 %multiply_subtract_fusion.252 = (f32[256]{0:T(256)S(1)}, f32[256]{0:T(256)S(1)}, f32[256]{0:T(256)S(1)}, f32[256]{0:T(256)S(1)}, f32[256]{0:T(256)S(1)}, /*index...) fusion(f32[256]{0:T(256)S(1)} %bitcast.3176, ...), kind=kLoop, calls=%fused_computation.99.clone.1 | loop fusion | flops 16384 | bytes 66688 | tf_op jit(solution)/shard_map/while/body/eval_jaxpr/sub | solution.py:45
  439.8 20.0 %multiply_subtract_fusion.252 = (f32[256]{0:T(256)S(1)}, f32[256]{0:T(256)S(1)}, f32[256]{0:T(256)S(1)}, f32[256]{0:T(256)S(1)}, f32[256]{0:T(256)S(1)}, /*index...) fusion(f32[256]{0:T(256)S(1)} %bitcast.3176, ...), kind=kLoop, calls=%fused_computation.99.clone.1 | loop fusion | flops 16384 | bytes 66688 | tf_op jit(solution)/shard_map/while/body/eval_jaxpr/sub | solution.py:45
  461.5 20.0 %multiply_subtract_fusion.252 = (f32[256]{0:T(256)S(1)}, f32[256]{0:T(256)S(1)}, f32[256]{0:T(256)S(1)}, f32[256]{0:T(256)S(1)}, f32[256]{0:T(256)S(1)}, /*index...) fusion(f32[256]{0:T(256)S(1)} %bitcast.3176, ...), kind=kLoop, calls=%fused_computation.99.clone.1 | loop fusion | flops 16384 | bytes 66688 | tf_op jit(solution)/shard_map/while/body/eval_jaxpr/sub | solution.py:45
  483.3 20.0 %multiply_subtract_fusion.252 = (f32[256]{0:T(256)S(1)}, f32[256]{0:T(256)S(1)}, f32[256]{0:T(256)S(1)}, f32[256]{0:T(256)S(1)}, f32[256]{0:T(256)S(1)}, /*index...) fusion(f32[256]{0:T(256)S(1)} %bitcast.3176, ...), kind=kLoop, calls=%fused_computation.99.clone.1 | loop fusion | flops 16384 | bytes 66688 | tf_op jit(solution)/shard_map/while/body/eval_jaxpr/sub | solution.py:45
  512.7 4.1 collective-permute-start.3
  526.0 10.4 %copy.124 = f32[3,8,1,4096]{1,2,0,3:T(1,128)} copy(f32[3,8,1,4096]{3,1,2,0:T(8,128)S(1)} %copy_add_fusion) | data formatting | bytes 786432 | tf_op jit(solution)/shard_map/add | solution.py:151
  536.9 22.9 %reduce.12 = f32[4096,3,8]{2,1,0:T(4,128)} reduce(f32[4096,3,1,8]{3,2,1,0:T(1,128)} %bitcast.2960, f32[]{:T(128)} %broadcast.790), dimensions={2}, to_apply=%bitcast.1784.reduce_sub_computation | reduce | bytes 786436
  559.8 9.1 %reshape.854 = f32[32,1,3072]{2,1,0:T(1,128)} reshape(f32[4096,3,8]{2,1,0:T(4,128)} %reduce.12) | data formatting | bytes 786432
  568.8 7.4 %all-to-all-start.1 = ((f32[32,1,3072]{2,1,0:T(1,128)}), f32[32,1,3072]{2,1,0:T(1,128)S(1)}, u32[]{:S(2)}, u32[]{:S(2)}) async-start(f32[32,1,3072]{2,1,0:T(1,128)} %reshape.854), calls=%async_computation.1 | async-start | bytes 786432 | tf_op jit(solution)/shard_map/all_to_all | solution.py:152
  577.2 7.8 %all-to-all-done.1 = f32[32,1,3072]{2,1,0:T(1,128)S(1)} async-done(((f32[32,1,3072]{2,1,0:T(1,128)}), f32[32,1,3072]{2,1,0:T(1,128)S(1)}, u32[]{:S(2)}, u32[]{:S(2)}) %all-to-all-start.1) | async-done | bytes 393248 | tf_op jit(solution)/shard_map/all_to_all | solution.py:152
  586.6 12.8 %reshape.855 = f32[4096,3,1,8]{3,2,1,0:T(1,128)} reshape(f32[32,3072]{1,0:T(8,128)S(1)} %reduce.13) | data formatting | bytes 786432
  599.7 12.3 %copy.125 = f32[3,8,1,4096]{3,2,1,0:T(1,128)S(1)} copy(f32[3,8,1,4096]{1,2,0,3:T(1,128)} %bitcast.2961) | data formatting | bytes 786432 | tf_op jit(solution)/shard_map/all_to_all | solution.py:152
  614.3 5.1 collective-permute-start.4
  619.7 19.3 %multiply_subtract_fusion.97 = (f32[256]{0:T(256)S(1)}, f32[256]{0:T(256)S(1)}, f32[256]{0:T(256)S(1)}, f32[256]{0:T(256)S(1)}, f32[256]{0:T(256)S(1)}, /*index=...) fusion(f32[256]{0:T(256)S(1)} %bitcast.3554, ...), kind=kLoop, calls=%fused_computation.660 | loop fusion | flops 15872 | bytes 64636 | tf_op jit(solution)/shard_map/eval_jaxpr/sub | solution.py:45
  646.8 2.9 collective-permute-start.7
  (453 shorter events, 95.8 us)
Async XLA Ops:
  2.0 514.9 %all-to-all-start = ((f32[3,256,1,128]{3,2,0,1:T(1,128)}), f32[3,256,1,128]{3,2,0,1:T(1,128)S(1)}, u32[]{:S(2)}, u32[]{:S(2)}) async-start(f32[3,256,1,128]{3,2,0,1:T(1,128)} %copy.113), calls=%async_computation | async-start | bytes 786432 | tf_op jit(solution)/shard_map/all_to_all | solution.py:147
  14.8 489.3 %collective-permute-start = (f32[6,3,1,128]{3,1,0,2:T(4,128)S(1)}, f32[6,3,1,128]{3,1,0,2:T(4,128)S(1)}, u32[]{:S(2)}, u32[]{:S(2)}) collective-permute-start(f32[6,3,1,128]{3,1,0,2:T(4,128)S(1)} %get-tuple-element.1127), channel_id=1, source_target_pairs={{32,0},{64,32},{96,64},{128,96},{160,128},{192,160},{224,192},{256... | collective-permute-start | bytes 27656 | tf_op jit(solution)/shard_map/ppermute | solution.py:22
  24.4 479.8 %collective-permute-start.1 = (f32[6,3,1,128]{3,1,0,2:T(4,128)S(1)}, f32[6,3,1,128]{3,1,0,2:T(4,128)S(1)}, u32[]{:S(2)}, u32[]{:S(2)}) collective-permute-start(f32[6,3,1,128]{3,1,0,2:T(4,128)S(1)} %get-tuple-element.1128), channel_id=1, source_target_pairs={{0,32},{32,64},{64,96},{96,128},{128,160},{160,192},{192,224},{224... | collective-permute-start | bytes 27656 | tf_op jit(solution)/shard_map/ppermute | solution.py:19
  32.2 100.7 %copy-start.8 = (f32[3,32,128]{2,1,0:T(8,128)}, f32[3,32,128]{2,1,0:T(8,128)S(1)}, u32[]{:S(2)}) copy-start(f32[3,32,128]{2,1,0:T(8,128)S(1)} %get-tuple-element.434) | copy-start | bytes 147460
  350.7 153.5 %copy-start = (f32[3,256,1,128]{3,2,1,0:T(1,128)S(1)}, f32[3,256,1,128]{3,2,1,0:T(1,128)}, u32[]{:S(2)}) copy-start(f32[3,256,1,128]{3,2,1,0:T(1,128)} %param.13) | copy-start | bytes 1179652
  503.4 13.5 %copy-start.4 = (f32[7,32,256]{2,1,0:T(8,128)}, f32[7,32,256]{2,1,0:T(8,128)S(1)}, u32[]{:S(2)}) copy-start(f32[7,32,256]{2,1,0:T(8,128)S(1)} %get-tuple-element.427) | copy-start | bytes 688132
  505.4 11.4 %copy-start.6 = (f32[6,256,1,128]{3,1,0,2:T(8,128)}, f32[6,256,1,128]{3,1,0,2:T(8,128)S(1)}, u32[]{:S(2)}) copy-start(f32[6,256,1,128]{3,1,0,2:T(8,128)S(1)} %convolution_bitcast_fusion) | copy-start | bytes 2359300
  505.4 6.7 %collective-permute-start.2 = (f32[6,1,1,128]{3,1,0,2:T(1,128)S(1)}, f32[6,1,1,128]{3,1,0,2:T(1,128)S(1)}, u32[]{:S(2)}, u32[]{:S(2)}) collective-permute-start(f32[6,1,1,128]{3,1,0,2:T(1,128)S(1)} %slice.4306), channel_id=1, source_target_pairs={{0,32},{32,64},{64,96},{96,128},{128,160},{160,192},{192,224},{224... | collective-permute-start | bytes 9224 | tf_op jit(solution)/shard_map/ppermute | solution.py:19
  512.7 63.5 %collective-permute-start.3 = (f32[6,1,1,128]{3,1,0,2:T(1,128)}, f32[6,1,1,128]{3,1,0,2:T(1,128)}, u32[]{:S(2)}, u32[]{:S(2)}) collective-permute-start(f32[6,1,1,128]{3,1,0,2:T(1,128)} %get-tuple-element.1124), channel_id=1, source_target_pairs={{32,0},{64,32},{96,64},{128,96},{160,128},{192,160},{224,192},{256... | collective-permute-start | bytes 9224 | tf_op jit(solution)/shard_map/ppermute | solution.py:22
  559.8 16.5 %copy-start.7 = (f32[6,256,1,128]{3,1,0,2:T(8,128)S(1)}, f32[6,256,1,128]{3,1,0,2:T(8,128)}, u32[]{:S(2)}) copy-start(f32[6,256,1,128]{3,1,0,2:T(8,128)} %copy-done.6) | copy-start | bytes 2359300
  568.8 16.2 %all-to-all-start.1 = ((f32[32,1,3072]{2,1,0:T(1,128)}), f32[32,1,3072]{2,1,0:T(1,128)S(1)}, u32[]{:S(2)}, u32[]{:S(2)}) async-start(f32[32,1,3072]{2,1,0:T(1,128)} %reshape.854), calls=%async_computation.1 | async-start | bytes 786432 | tf_op jit(solution)/shard_map/all_to_all | solution.py:152
  599.4 12.6 %copy-start.2 = (f32[1,256,1,128]{3,2,1,0:T(1,128)S(1)}, f32[1,256,1,128]{3,2,1,0:T(1,128)}, u32[]{:S(2)}) copy-start(f32[1,256,1,128]{3,2,1,0:T(1,128)} %copy-done.1) | copy-start | bytes 393220
  599.4 20.0 %copy-start.9 = (f32[1,256]{1,0:T(1,128)S(1)}, f32[1,256]{1,0:T(1,128)}, u32[]{:S(2)}) copy-start(f32[1,256]{1,0:T(1,128)} %get-tuple-element.1188) | copy-start | bytes 3076
  599.4 20.0 %copy-start.10 = (f32[1,256]{1,0:T(1,128)S(1)}, f32[1,256]{1,0:T(1,128)}, u32[]{:S(2)}) copy-start(f32[1,256]{1,0:T(1,128)} %get-tuple-element.1189) | copy-start | bytes 3076
  599.4 20.0 %copy-start.11 = (f32[1,256]{1,0:T(1,128)S(1)}, f32[1,256]{1,0:T(1,128)}, u32[]{:S(2)}) copy-start(f32[1,256]{1,0:T(1,128)} %get-tuple-element.1190) | copy-start | bytes 3076
  599.4 20.0 %copy-start.12 = (f32[1,256]{1,0:T(1,128)S(1)}, f32[1,256]{1,0:T(1,128)}, u32[]{:S(2)}) copy-start(f32[1,256]{1,0:T(1,128)} %get-tuple-element.1191) | copy-start | bytes 3076
  599.4 20.0 %copy-start.13 = (f32[1,256]{1,0:T(1,128)S(1)}, f32[1,256]{1,0:T(1,128)}, u32[]{:S(2)}) copy-start(f32[1,256]{1,0:T(1,128)} %get-tuple-element.1192) | copy-start | bytes 3076
  599.4 20.0 %copy-start.14 = (f32[1,256]{1,0:T(1,128)S(1)}, f32[1,256]{1,0:T(1,128)}, u32[]{:S(2)}) copy-start(f32[1,256]{1,0:T(1,128)} %get-tuple-element.1193) | copy-start | bytes 3076
  599.4 20.0 %copy-start.15 = (f32[1,256]{1,0:T(1,128)S(1)}, f32[1,256]{1,0:T(1,128)}, u32[]{:S(2)}) copy-start(f32[1,256]{1,0:T(1,128)} %get-tuple-element.1194) | copy-start | bytes 3076
  599.5 20.0 %copy-start.16 = (f32[1,256]{1,0:T(1,128)S(1)}, f32[1,256]{1,0:T(1,128)}, u32[]{:S(2)}) copy-start(f32[1,256]{1,0:T(1,128)} %get-tuple-element.1195) | copy-start | bytes 3076
  599.5 20.0 %copy-start.17 = (f32[1,256]{1,0:T(1,128)S(1)}, f32[1,256]{1,0:T(1,128)}, u32[]{:S(2)}) copy-start(f32[1,256]{1,0:T(1,128)} %get-tuple-element.1196) | copy-start | bytes 3076
  599.5 20.0 %copy-start.18 = (f32[1,256]{1,0:T(1,128)S(1)}, f32[1,256]{1,0:T(1,128)}, u32[]{:S(2)}) copy-start(f32[1,256]{1,0:T(1,128)} %get-tuple-element.1197) | copy-start | bytes 3076
  599.5 20.0 %copy-start.19 = (f32[1,256]{1,0:T(1,128)S(1)}, f32[1,256]{1,0:T(1,128)}, u32[]{:S(2)}) copy-start(f32[1,256]{1,0:T(1,128)} %get-tuple-element.1198) | copy-start | bytes 3076
  599.5 20.0 %copy-start.20 = (f32[1,256]{1,0:T(1,128)S(1)}, f32[1,256]{1,0:T(1,128)}, u32[]{:S(2)}) copy-start(f32[1,256]{1,0:T(1,128)} %get-tuple-element.1199) | copy-start | bytes 3076
  599.5 20.0 %copy-start.21 = (f32[1,256]{1,0:T(1,128)S(1)}, f32[1,256]{1,0:T(1,128)}, u32[]{:S(2)}) copy-start(f32[1,256]{1,0:T(1,128)} %get-tuple-element.1169) | copy-start | bytes 3076
  599.5 20.0 %copy-start.22 = (f32[1,256]{1,0:T(1,128)S(1)}, f32[1,256]{1,0:T(1,128)}, u32[]{:S(2)}) copy-start(f32[1,256]{1,0:T(1,128)} %get-tuple-element.1170) | copy-start | bytes 3076
  599.5 20.0 %copy-start.23 = (f32[1,256]{1,0:T(1,128)S(1)}, f32[1,256]{1,0:T(1,128)}, u32[]{:S(2)}) copy-start(f32[1,256]{1,0:T(1,128)} %get-tuple-element.1171) | copy-start | bytes 3076
  599.5 20.0 %copy-start.24 = (f32[1,256]{1,0:T(1,128)S(1)}, f32[1,256]{1,0:T(1,128)}, u32[]{:S(2)}) copy-start(f32[1,256]{1,0:T(1,128)} %get-tuple-element.1172) | copy-start | bytes 3076
  599.5 20.0 %copy-start.25 = (f32[1,256]{1,0:T(1,128)S(1)}, f32[1,256]{1,0:T(1,128)}, u32[]{:S(2)}) copy-start(f32[1,256]{1,0:T(1,128)} %get-tuple-element.1173) | copy-start | bytes 3076
  599.6 20.0 %copy-start.26 = (f32[1,256]{1,0:T(1,128)S(1)}, f32[1,256]{1,0:T(1,128)}, u32[]{:S(2)}) copy-start(f32[1,256]{1,0:T(1,128)} %get-tuple-element.1174) | copy-start | bytes 3076
  599.6 20.0 %copy-start.27 = (f32[1,256]{1,0:T(1,128)S(1)}, f32[1,256]{1,0:T(1,128)}, u32[]{:S(2)}) copy-start(f32[1,256]{1,0:T(1,128)} %get-tuple-element.1175) | copy-start | bytes 3076
  599.6 20.0 %copy-start.28 = (f32[1,256]{1,0:T(1,128)S(1)}, f32[1,256]{1,0:T(1,128)}, u32[]{:S(2)}) copy-start(f32[1,256]{1,0:T(1,128)} %get-tuple-element.1176) | copy-start | bytes 3076
  599.6 20.0 %copy-start.29 = (f32[1,256]{1,0:T(1,128)S(1)}, f32[1,256]{1,0:T(1,128)}, u32[]{:S(2)}) copy-start(f32[1,256]{1,0:T(1,128)} %get-tuple-element.1177) | copy-start | bytes 3076
  599.6 20.0 %copy-start.30 = (f32[1,256]{1,0:T(1,128)S(1)}, f32[1,256]{1,0:T(1,128)}, u32[]{:S(2)}) copy-start(f32[1,256]{1,0:T(1,128)} %get-tuple-element.1178) | copy-start | bytes 3076
  599.6 20.0 %copy-start.31 = (f32[1,256]{1,0:T(1,128)S(1)}, f32[1,256]{1,0:T(1,128)}, u32[]{:S(2)}) copy-start(f32[1,256]{1,0:T(1,128)} %get-tuple-element.1179) | copy-start | bytes 3076
  599.6 20.0 %copy-start.32 = (f32[1,256]{1,0:T(1,128)S(1)}, f32[1,256]{1,0:T(1,128)}, u32[]{:S(2)}) copy-start(f32[1,256]{1,0:T(1,128)} %get-tuple-element.1180) | copy-start | bytes 3076
  599.6 20.0 %copy-start.33 = (f32[1,256]{1,0:T(1,128)S(1)}, f32[1,256]{1,0:T(1,128)}, u32[]{:S(2)}) copy-start(f32[1,256]{1,0:T(1,128)} %get-tuple-element.1181) | copy-start | bytes 3076
  599.6 20.0 %copy-start.34 = (f32[1,256]{1,0:T(1,128)S(1)}, f32[1,256]{1,0:T(1,128)}, u32[]{:S(2)}) copy-start(f32[1,256]{1,0:T(1,128)} %get-tuple-element.1182) | copy-start | bytes 3076
  599.6 20.0 %copy-start.35 = (f32[1,256]{1,0:T(1,128)S(1)}, f32[1,256]{1,0:T(1,128)}, u32[]{:S(2)}) copy-start(f32[1,256]{1,0:T(1,128)} %get-tuple-element.1183) | copy-start | bytes 3076
  599.7 20.0 %copy-start.36 = (f32[1,256]{1,0:T(1,128)S(1)}, f32[1,256]{1,0:T(1,128)}, u32[]{:S(2)}) copy-start(f32[1,256]{1,0:T(1,128)} %get-tuple-element.1184) | copy-start | bytes 3076
  599.7 20.0 %copy-start.37 = (f32[1,256]{1,0:T(1,128)S(1)}, f32[1,256]{1,0:T(1,128)}, u32[]{:S(2)}) copy-start(f32[1,256]{1,0:T(1,128)} %get-tuple-element.1185) | copy-start | bytes 3076
  599.7 20.0 %copy-start.38 = (f32[1,256]{1,0:T(1,128)S(1)}, f32[1,256]{1,0:T(1,128)}, u32[]{:S(2)}) copy-start(f32[1,256]{1,0:T(1,128)} %get-tuple-element.1186) | copy-start | bytes 3076
  599.7 20.0 %copy-start.39 = (f32[1,256]{1,0:T(1,128)S(1)}, f32[1,256]{1,0:T(1,128)}, u32[]{:S(2)}) copy-start(f32[1,256]{1,0:T(1,128)} %get-tuple-element.1187) | copy-start | bytes 3076
  599.7 39.4 %copy-start.5 = (f32[7,32,256]{2,1,0:T(8,128)S(1)}, f32[7,32,256]{2,1,0:T(8,128)}, u32[]{:S(2)}) copy-start(f32[7,32,256]{2,1,0:T(8,128)} %copy-done.4) | copy-start | bytes 688132
  612.3 26.8 %collective-permute-start.5 = (f32[3,3,1,128]{3,1,0,2:T(4,128)S(1)}, f32[3,3,1,128]{3,1,0,2:T(4,128)S(1)}, u32[]{:S(2)}, u32[]{:S(2)}) collective-permute-start(f32[3,3,1,128]{3,1,0,2:T(4,128)S(1)} %get-tuple-element.1134), channel_id=1, source_target_pairs={{0,32},{32,64},{64,96},{96,128},{128,160},{160,192},{192,224},{224... | collective-permute-start | bytes 13832 | tf_op jit(solution)/shard_map/ppermute | solution.py:19
  614.3 24.9 %collective-permute-start.4 = (f32[3,3,1,128]{3,1,0,2:T(4,128)S(1)}, f32[3,3,1,128]{3,1,0,2:T(4,128)S(1)}, u32[]{:S(2)}, u32[]{:S(2)}) collective-permute-start(f32[3,3,1,128]{3,1,0,2:T(4,128)S(1)} %get-tuple-element.1133), channel_id=1, source_target_pairs={{32,0},{64,32},{96,64},{128,96},{160,128},{192,160},{224,192},{256... | collective-permute-start | bytes 13832 | tf_op jit(solution)/shard_map/ppermute | solution.py:22
  640.1 6.7 %collective-permute-start.6 = (f32[3,1,1,128]{3,1,0,2:T(1,128)S(1)}, f32[3,1,1,128]{3,1,0,2:T(1,128)S(1)}, u32[]{:S(2)}, u32[]{:S(2)}) collective-permute-start(f32[3,1,1,128]{3,1,0,2:T(1,128)S(1)} %slice.4403), channel_id=1, source_target_pairs={{0,32},{32,64},{64,96},{96,128},{128,160},{160,192},{192,224},{224... | collective-permute-start | bytes 4616 | tf_op jit(solution)/shard_map/ppermute | solution.py:19
  646.8 5.5 collective-permute-start.7
  (2 other events, 1.3 us)
where the time goes:
time: 661 us; the launch traced here: 653 us
  other arithmetic  457 us (69%)
  local copies, waits for them, and re-layouts  97.7 us (15%)
  starting transfers between devices  46.2 us (7%)
  loops' own time  25.7 us (4%)
  waiting for transfers between devices  14.1 us (2%)
  between operations  8.93 us (1%)
    sub x19, other arithmetic, tables(): lax.linalg.tridiagonal_solve(lower_diag, main_diag, upper_diag, identity)  379 us
    broadcast_in_dim x17, other arithmetic, tables(): lax.linalg.tridiagonal_solve(lower_diag, main_diag, upper_diag, identity)  40.6 us
    slice x110, local copies, waits for them, and re-layouts, tables(): lax.linalg.tridiagonal_solve(lower_diag, main_diag, upper_diag, identity)  35.7 us
    another operation x6, loops' own time, tables(): lax.linalg.tridiagonal_solve(lower_diag, main_diag, upper_diag, identity)  25.7 us
    unnamed x89, local copies, waits for them, and re-layouts  25.6 us
    unnamed x1, other arithmetic  22.9 us
    ppermute x4, starting transfers between devices, with_halo(): lax.ppermute(lax.slice_in_dim(block, 0, width, axis=dim), axis, backward)  21.7 us
  transfers between devices with their start and end apart: 10, of which 4 were waited for; matrix products, arithmetic and copies ran while one was open for 81% of the time, Pallas kernels for 0%

commit v1 on v0

--- a/solution.py
+++ b/solution.py
@@ -149,7 +149,10 @@
     fields = jnp.concatenate([pencil, along_z * pencil], axis=0)
     slopes = solve_blocks(slope_rhs(wrap_pad(fields, 3), fields.shape[3], 3), slope_z)
     local_terms = slopes[3:] + along_z * slopes[:3]
-    return lax.all_to_all(local_terms, "gz", split_axis=3, concat_axis=1, tiled=True)
+    return jnp.concatenate(
+        lax.all_to_all(jnp.stack(jnp.split(local_terms, lax.axis_size("gz"), axis=3)), "gz", 0, 0),
+        axis=1,
+    )
 
 
 def per_device(velocity):

time: 661 us -> 624 us (0.944)
  local copies, waits for them, and re-layouts: 97.7 us -> 72.8 us
  other arithmetic: 457 us -> 447 us
    unnamed x1 -> x0, other arithmetic: 22.9 us -> none
    all_to_all x1 -> x0, local copies, waits for them, and re-layouts: 12.3 us -> none  [z_part(): lax.all_to_all(local_terms, 'gz', split_axis=3, concat_axis=1, tiled=True)]
    add x1 -> x0, local copies, waits for them, and re-layouts: 10.4 us -> none  [z_part(): local_terms = slopes[3:] + along_z * slopes[:3]]
    add x0 -> x1, other arithmetic: none -> 6.65 us  [slope_rhs(): rhs + COEF_B * 0.25 * (offset_slice(extended, 2, length, direction, base)...]
    unnamed x89 -> x73, local copies, waits for them, and re-layouts: 25.6 us -> 20.7 us
  transfers between devices with their start and end apart: 10 -> 10, of which waited for: 4 -> 4; matrix products, arithmetic and copies ran while one was open for 81% -> 84% of each run, Pallas kernels for 0% -> 0%
where the time goes in v1:
time: 624 us; the launch traced here: 617 us
  other arithmetic  447 us (72%)
  local copies, waits for them, and re-layouts  72.8 us (12%)
  starting transfers between devices  45.7 us (7%)
  loops' own time  25.8 us (4%)
  waiting for transfers between devices  13.3 us (2%)
  between operations  8.81 us (1%)
    sub x19, other arithmetic, tables(): lax.linalg.tridiagonal_solve(lower_diag, main_diag, upper_diag, identity)  383 us
    broadcast_in_dim x17, other arithmetic, tables(): lax.linalg.tridiagonal_solve(lower_diag, main_diag, upper_diag, identity)  40.6 us
    slice x110, local copies, waits for them, and re-layouts, tables(): lax.linalg.tridiagonal_solve(lower_diag, main_diag, upper_diag, identity)  36.2 us
    another operation x6, loops' own time, tables(): lax.linalg.tridiagonal_solve(lower_diag, main_diag, upper_diag, identity)  25.8 us
    ppermute x4, starting transfers between devices, with_halo(): lax.ppermute(lax.slice_in_dim(block, 0, width, axis=dim), axis, backward)  20.9 us
    unnamed x73, local copies, waits for them, and re-layouts  20.7 us
  transfers between devices with their start and end apart: 10, of which 4 were waited for; matrix products, arithmetic and copies ran while one was open for 84% of the time, Pallas kernels for 0%

profile of v1, /device:TPU:2, one launch (start us, length us, event | category | flops | bytes accessed | tf_op | source)
XLA Modules:
  0.0 617.3 jit_solution(1798751698362468421)
XLA Ops:
  2.0 9.5 %all-to-all-start = ((f32[3,256,1,128]{3,2,0,1:T(1,128)}), f32[3,256,1,128]{3,2,0,1:T(1,128)S(1)}, u32[]{:S(2)}, u32[]{:S(2)}) async-start(f32[3,256,1,128]{3,2,0,1:T(1,128)} %copy.150), calls=%async_computation | async-start | bytes 786432 | tf_op jit(solution)/shard_map/all_to_all | solution.py:147
  14.2 9.6 %collective-permute-start = (f32[6,3,1,128]{3,1,0,2:T(4,128)S(1)}, f32[6,3,1,128]{3,1,0,2:T(4,128)S(1)}, u32[]{:S(2)}, u32[]{:S(2)}) collective-permute-start(f32[6,3,1,128]{3,1,0,2:T(4,128)S(1)} %get-tuple-element.1127), channel_id=1, source_target_pairs={{32,0},{64,32},{96,64},{128,96},{160,128},{192,160},{224,192},{256... | collective-permute-start | bytes 27656 | tf_op jit(solution)/shard_map/ppermute | solution.py:22
  25.9 14.9 %while.96 = (s32[]{:T(128)}, f32[]{:T(128)}, f32[256]{0:T(256)S(1)}, f32[7,32]{1,0:T(8,128)S(1)}, f32[7,32,256]{2,1,0:T(8,128)S(1)}, /*index=5*/f32[7,32,256]{2,...) while((s32[]{:T(128)}, f32[]{:T(128)}, ...), condition=%wide.region_1.2_spmd, body=%wide.region_0.1_spmd.sunk | while | flops 24705 | bytes 267869 | solution.py:45
  42.2 5.9 while.100
  49.6 14.9 %while.98 = (s32[]{:T(128)}, f32[]{:T(128)}, f32[256]{0:T(256)S(1)}, f32[7,32]{1,0:T(8,128)S(1)}, f32[7,32,256]{2,1,0:T(8,128)S(1)}, /*index=5*/f32[7,32,256]{2,...) while((s32[]{:T(128)}, f32[]{:T(128)}, ...), condition=%wide.region_5.6_spmd, body=%wide.region_4.5_spmd.sunk | while | flops 24705 | bytes 267869 | solution.py:45
  68.1 154.3 %while.97 = (s32[]{:T(128)}, f32[256]{0:T(256)S(1)}, f32[7,32,256]{2,1,0:T(8,128)S(1)}, f32[7,32,256]{2,1,0:T(8,128)S(1)}, f32[7,32]{1,0:T(8,128)S(1)}, /*index=...) while((s32[]{:T(128)}, f32[256]{0:T(256)S(1)}, ...), condition=%wide.region_3.4_spmd, body=%wide.region_2.3_spmd.sunk | while | flops 16418 | bytes 266713 | solution.py:45
  69.8 20.2 %multiply_subtract_fusion.252 = (f32[256]{0:T(256)S(1)}, f32[256]{0:T(256)S(1)}, f32[256]{0:T(256)S(1)}, f32[256]{0:T(256)S(1)}, f32[256]{0:T(256)S(1)}, /*index...) fusion(f32[256]{0:T(256)S(1)} %bitcast.3249, ...), kind=kLoop, calls=%fused_computation.99.clone.1 | loop fusion | flops 16384 | bytes 66688 | tf_op jit(solution)/shard_map/while/body/eval_jaxpr/sub | solution.py:45
  91.8 20.2 %multiply_subtract_fusion.252 = (f32[256]{0:T(256)S(1)}, f32[256]{0:T(256)S(1)}, f32[256]{0:T(256)S(1)}, f32[256]{0:T(256)S(1)}, f32[256]{0:T(256)S(1)}, /*index...) fusion(f32[256]{0:T(256)S(1)} %bitcast.3249, ...), kind=kLoop, calls=%fused_computation.99.clone.1 | loop fusion | flops 16384 | bytes 66688 | tf_op jit(solution)/shard_map/while/body/eval_jaxpr/sub | solution.py:45
  113.9 20.2 %multiply_subtract_fusion.252 = (f32[256]{0:T(256)S(1)}, f32[256]{0:T(256)S(1)}, f32[256]{0:T(256)S(1)}, f32[256]{0:T(256)S(1)}, f32[256]{0:T(256)S(1)}, /*index...) fusion(f32[256]{0:T(256)S(1)} %bitcast.3249, ...), kind=kLoop, calls=%fused_computation.99.clone.1 | loop fusion | flops 16384 | bytes 66688 | tf_op jit(solution)/shard_map/while/body/eval_jaxpr/sub | solution.py:45
  135.9 20.2 %multiply_subtract_fusion.252 = (f32[256]{0:T(256)S(1)}, f32[256]{0:T(256)S(1)}, f32[256]{0:T(256)S(1)}, f32[256]{0:T(256)S(1)}, f32[256]{0:T(256)S(1)}, /*index...) fusion(f32[256]{0:T(256)S(1)} %bitcast.3249, ...), kind=kLoop, calls=%fused_computation.99.clone.1 | loop fusion | flops 16384 | bytes 66688 | tf_op jit(solution)/shard_map/while/body/eval_jaxpr/sub | solution.py:45
  158.0 20.2 %multiply_subtract_fusion.252 = (f32[256]{0:T(256)S(1)}, f32[256]{0:T(256)S(1)}, f32[256]{0:T(256)S(1)}, f32[256]{0:T(256)S(1)}, f32[256]{0:T(256)S(1)}, /*index...) fusion(f32[256]{0:T(256)S(1)} %bitcast.3249, ...), kind=kLoop, calls=%fused_computation.99.clone.1 | loop fusion | flops 16384 | bytes 66688 | tf_op jit(solution)/shard_map/while/body/eval_jaxpr/sub | solution.py:45
  180.0 20.2 %multiply_subtract_fusion.252 = (f32[256]{0:T(256)S(1)}, f32[256]{0:T(256)S(1)}, f32[256]{0:T(256)S(1)}, f32[256]{0:T(256)S(1)}, f32[256]{0:T(256)S(1)}, /*index...) fusion(f32[256]{0:T(256)S(1)} %bitcast.3249, ...), kind=kLoop, calls=%fused_computation.99.clone.1 | loop fusion | flops 16384 | bytes 66688 | tf_op jit(solution)/shard_map/while/body/eval_jaxpr/sub | solution.py:45
  202.0 20.2 %multiply_subtract_fusion.252 = (f32[256]{0:T(256)S(1)}, f32[256]{0:T(256)S(1)}, f32[256]{0:T(256)S(1)}, f32[256]{0:T(256)S(1)}, f32[256]{0:T(256)S(1)}, /*index...) fusion(f32[256]{0:T(256)S(1)} %bitcast.3249, ...), kind=kLoop, calls=%fused_computation.99.clone.1 | loop fusion | flops 16384 | bytes 66688 | tf_op jit(solution)/shard_map/while/body/eval_jaxpr/sub | solution.py:45
  224.2 65.4 %while.101 = (s32[]{:T(128)}, f32[128]{0:T(128)S(1)}, f32[3,32,128]{2,1,0:T(8,128)S(1)}, f32[3,32,128]{2,1,0:T(8,128)S(1)}, f32[3,32]{1,0:T(4,128)S(1)}, /*index...) while((s32[]{:T(128)}, f32[128]{0:T(128)S(1)}, ...), condition=%wide.region_11.12_spmd, body=%wide.region_10.11_spmd.sunk | while | flops 8226 | bytes 101333 | solution.py:45
  225.7 20.2 %fusion.492 = (f32[128]{0:T(128)S(1)}, f32[128]{0:T(128)S(1)}, f32[128]{0:T(128)S(1)}, f32[128]{0:T(128)S(1)}, f32[128]{0:T(128)S(1)}, /*index=5*/f32[128]{0:T(1...) fusion(f32[3,32,128]{2,1,0:T(8,128)S(1)} %get-tuple-element.283, ...), kind=kLoop, calls=%fused_computation.428.clone.1 | loop fusion | flops 8192 | bytes 33536 | tf_op jit(solution)/shard_map/while/body/eval_jaxpr/sub | solution.py:45
  247.5 20.2 %fusion.492 = (f32[128]{0:T(128)S(1)}, f32[128]{0:T(128)S(1)}, f32[128]{0:T(128)S(1)}, f32[128]{0:T(128)S(1)}, f32[128]{0:T(128)S(1)}, /*index=5*/f32[128]{0:T(1...) fusion(f32[3,32,128]{2,1,0:T(8,128)S(1)} %get-tuple-element.283, ...), kind=kLoop, calls=%fused_computation.428.clone.1 | loop fusion | flops 8192 | bytes 33536 | tf_op jit(solution)/shard_map/while/body/eval_jaxpr/sub | solution.py:45
  269.3 20.2 %fusion.492 = (f32[128]{0:T(128)S(1)}, f32[128]{0:T(128)S(1)}, f32[128]{0:T(128)S(1)}, f32[128]{0:T(128)S(1)}, f32[128]{0:T(128)S(1)}, /*index=5*/f32[128]{0:T(1...) fusion(f32[3,32,128]{2,1,0:T(8,128)S(1)} %get-tuple-element.283, ...), kind=kLoop, calls=%fused_computation.428.clone.1 | loop fusion | flops 8192 | bytes 33536 | tf_op jit(solution)/shard_map/while/body/eval_jaxpr/sub | solution.py:45
  290.8 2.7 fusion.341
  293.5 2.7 fusion.340
  296.2 2.7 fusion.339
  298.9 2.7 fusion.338
  301.6 2.7 fusion.337
  304.2 2.6 fusion.336
  306.9 2.5 fusion.335
  309.4 2.6 fusion.334
  312.0 2.7 fusion.333
  314.7 2.7 fusion.332
  317.4 2.7 fusion.331
  320.0 2.6 fusion.330
  322.6 2.8 fusion.329
  325.4 2.8 fusion.328
  333.0 153.8 %while.99 = (s32[]{:T(128)}, f32[256]{0:T(256)S(1)}, f32[7,32,256]{2,1,0:T(8,128)S(1)}, f32[7,32,256]{2,1,0:T(8,128)S(1)}, f32[7,32]{1,0:T(8,128)S(1)}, /*index=...) while((s32[]{:T(128)}, f32[256]{0:T(256)S(1)}, ...), condition=%wide.region_7.8_spmd, body=%wide.region_6.7_spmd.sunk | while | flops 16418 | bytes 266713 | solution.py:45
  334.7 20.2 %multiply_subtract_fusion.253 = (f32[256]{0:T(256)S(1)}, f32[256]{0:T(256)S(1)}, f32[256]{0:T(256)S(1)}, f32[256]{0:T(256)S(1)}, f32[256]{0:T(256)S(1)}, /*index...) fusion(f32[256]{0:T(256)S(1)} %bitcast.3267, ...), kind=kLoop, calls=%fused_computation.230.clone.1 | loop fusion | flops 16384 | bytes 66688 | tf_op jit(solution)/shard_map/while/body/eval_jaxpr/sub | solution.py:45
  356.6 20.2 %multiply_subtract_fusion.253 = (f32[256]{0:T(256)S(1)}, f32[256]{0:T(256)S(1)}, f32[256]{0:T(256)S(1)}, f32[256]{0:T(256)S(1)}, f32[256]{0:T(256)S(1)}, /*index...) fusion(f32[256]{0:T(256)S(1)} %bitcast.3267, ...), kind=kLoop, calls=%fused_computation.230.clone.1 | loop fusion | flops 16384 | bytes 66688 | tf_op jit(solution)/shard_map/while/body/eval_jaxpr/sub | solution.py:45
  378.6 20.2 %multiply_subtract_fusion.253 = (f32[256]{0:T(256)S(1)}, f32[256]{0:T(256)S(1)}, f32[256]{0:T(256)S(1)}, f32[256]{0:T(256)S(1)}, f32[256]{0:T(256)S(1)}, /*index...) fusion(f32[256]{0:T(256)S(1)} %bitcast.3267, ...), kind=kLoop, calls=%fused_computation.230.clone.1 | loop fusion | flops 16384 | bytes 66688 | tf_op jit(solution)/shard_map/while/body/eval_jaxpr/sub | solution.py:45
  400.6 20.2 %multiply_subtract_fusion.253 = (f32[256]{0:T(256)S(1)}, f32[256]{0:T(256)S(1)}, f32[256]{0:T(256)S(1)}, f32[256]{0:T(256)S(1)}, f32[256]{0:T(256)S(1)}, /*index...) fusion(f32[256]{0:T(256)S(1)} %bitcast.3267, ...), kind=kLoop, calls=%fused_computation.230.clone.1 | loop fusion | flops 16384 | bytes 66688 | tf_op jit(solution)/shard_map/while/body/eval_jaxpr/sub | solution.py:45
  422.5 20.2 %multiply_subtract_fusion.253 = (f32[256]{0:T(256)S(1)}, f32[256]{0:T(256)S(1)}, f32[256]{0:T(256)S(1)}, f32[256]{0:T(256)S(1)}, f32[256]{0:T(256)S(1)}, /*index...) fusion(f32[256]{0:T(256)S(1)} %bitcast.3267, ...), kind=kLoop, calls=%fused_computation.230.clone.1 | loop fusion | flops 16384 | bytes 66688 | tf_op jit(solution)/shard_map/while/body/eval_jaxpr/sub | solution.py:45
  444.5 20.2 %multiply_subtract_fusion.253 = (f32[256]{0:T(256)S(1)}, f32[256]{0:T(256)S(1)}, f32[256]{0:T(256)S(1)}, f32[256]{0:T(256)S(1)}, f32[256]{0:T(256)S(1)}, /*index...) fusion(f32[256]{0:T(256)S(1)} %bitcast.3267, ...), kind=kLoop, calls=%fused_computation.230.clone.1 | loop fusion | flops 16384 | bytes 66688 | tf_op jit(solution)/shard_map/while/body/eval_jaxpr/sub | solution.py:45
  466.5 20.2 %multiply_subtract_fusion.253 = (f32[256]{0:T(256)S(1)}, f32[256]{0:T(256)S(1)}, f32[256]{0:T(256)S(1)}, f32[256]{0:T(256)S(1)}, f32[256]{0:T(256)S(1)}, /*index...) fusion(f32[256]{0:T(256)S(1)} %bitcast.3267, ...), kind=kLoop, calls=%fused_computation.230.clone.1 | loop fusion | flops 16384 | bytes 66688 | tf_op jit(solution)/shard_map/while/body/eval_jaxpr/sub | solution.py:45
  486.8 19.4 %multiply_subtract_fusion.66 = (f32[256]{0:T(256)S(1)}, f32[256]{0:T(256)S(1)}, f32[256]{0:T(256)S(1)}, f32[256]{0:T(256)S(1)}, f32[256]{0:T(256)S(1)}, /*index=...) fusion(f32[256]{0:T(256)S(1)} %bitcast.3727, ...), kind=kLoop, calls=%fused_computation.627 | loop fusion | flops 15872 | bytes 64636 | tf_op jit(solution)/shard_map/eval_jaxpr/sub | solution.py:45
  515.9 4.1 collective-permute-start.3
  522.0 4.2 fusion.161
  526.2 6.6 %fusion.163 = f32[6,8,1,4096]{3,2,1,0:T(1,128)S(1)} fusion(f32[6,8,1,4099]{3,2,1,0:T(1,128)S(1)} %get-tuple-element.1130, f32[6,8,1,4099]{3,2,1,0:T(1,128)S(1)} %get-tuple-element.1129), kind=kLoop, calls=%fused_computation.500 | loop fusion | flops 983040 | bytes 3932160 | tf_op jit(solution)/shard_map/add | solution.py:65
  560.6 7.4 %all-to-all-start.1 = ((f32[32,3,8,1,128]{4,2,1,3,0:T(8,128)}), f32[32,3,8,1,128]{4,2,1,3,0:T(8,128)S(1)}, u32[]{:S(2)}, u32[]{:S(2)}) async-start(f32[32,3,8,1,128]{4,2,1,3,0:T(8,128)} %constant_dynamic-update-slice_fusion), calls=%async_computation.1 | async-start | bytes 786432 | tf_op jit(solution)/shard_map/all_to_all | solution.py:153
  568.9 7.8 %all-to-all-done.1 = f32[32,3,8,1,128]{4,2,1,3,0:T(8,128)S(1)} async-done(((f32[32,3,8,1,128]{4,2,1,3,0:T(8,128)}), f32[32,3,8,1,128]{4,2,1,3,0:T(8,128)S(1)}, u32[]{:S(2)}, u32[]{:S(2)}) %all-to-all-start.1) | async-done | bytes 393248 | tf_op jit(solution)/shard_map/all_to_all | solution.py:153
  576.9 3.6 collective-permute-start.4
  582.8 20.3 %multiply_subtract_fusion.97 = (f32[256]{0:T(256)S(1)}, f32[256]{0:T(256)S(1)}, f32[256]{0:T(256)S(1)}, f32[256]{0:T(256)S(1)}, f32[256]{0:T(256)S(1)}, /*index=...) fusion(f32[256]{0:T(256)} %bitcast.3696, ...), kind=kLoop, calls=%fused_computation.689 | loop fusion | flops 15872 | bytes 64636 | tf_op jit(solution)/shard_map/eval_jaxpr/sub | solution.py:45
  610.9 3.6 collective-permute-start.7
  (436 shorter events, 105.9 us)
Async XLA Ops:
  2.0 518.0 %all-to-all-start = ((f32[3,256,1,128]{3,2,0,1:T(1,128)}), f32[3,256,1,128]{3,2,0,1:T(1,128)S(1)}, u32[]{:S(2)}, u32[]{:S(2)}) async-start(f32[3,256,1,128]{3,2,0,1:T(1,128)} %copy.150), calls=%async_computation | async-start | bytes 786432 | tf_op jit(solution)/shard_map/all_to_all | solution.py:147
  12.4 13.3 %copy-start.1 = (f32[1,256,1,128]{3,2,1,0:T(1,128)}, f32[1,256,1,128]{3,2,1,0:T(1,128)S(1)}, u32[]{:S(2)}) copy-start(f32[1,256,1,128]{3,2,1,0:T(1,128)S(1)} %slice.4060) | copy-start | bytes 393220
  14.2 493.0 %collective-permute-start = (f32[6,3,1,128]{3,1,0,2:T(4,128)S(1)}, f32[6,3,1,128]{3,1,0,2:T(4,128)S(1)}, u32[]{:S(2)}, u32[]{:S(2)}) collective-permute-start(f32[6,3,1,128]{3,1,0,2:T(4,128)S(1)} %get-tuple-element.1127), channel_id=1, source_target_pairs={{32,0},{64,32},{96,64},{128,96},{160,128},{192,160},{224,192},{256... | collective-permute-start | bytes 27656 | tf_op jit(solution)/shard_map/ppermute | solution.py:22
  23.8 483.5 %collective-permute-start.1 = (f32[6,3,1,128]{3,1,0,2:T(4,128)S(1)}, f32[6,3,1,128]{3,1,0,2:T(4,128)S(1)}, u32[]{:S(2)}, u32[]{:S(2)}) collective-permute-start(f32[6,3,1,128]{3,1,0,2:T(4,128)S(1)} %get-tuple-element.1128), channel_id=1, source_target_pairs={{0,32},{32,64},{64,96},{96,128},{128,160},{160,192},{192,224},{224... | collective-permute-start | bytes 27656 | tf_op jit(solution)/shard_map/ppermute | solution.py:19
  48.1 241.6 %copy-start.7 = (f32[3,32,128]{2,1,0:T(8,128)}, f32[3,32,128]{2,1,0:T(8,128)S(1)}, u32[]{:S(2)}) copy-start(f32[3,32,128]{2,1,0:T(8,128)S(1)} %get-tuple-element.434) | copy-start | bytes 147460
  222.4 107.9 %copy-start.3 = (f32[7,32,256]{2,1,0:T(8,128)}, f32[7,32,256]{2,1,0:T(8,128)S(1)}, u32[]{:S(2)}) copy-start(f32[7,32,256]{2,1,0:T(8,128)S(1)} %get-tuple-element.427) | copy-start | bytes 688132
  333.0 174.3 %copy-start = (f32[3,256,1,128]{3,2,1,0:T(1,128)S(1)}, f32[3,256,1,128]{3,2,1,0:T(1,128)}, u32[]{:S(2)}) copy-start(f32[3,256,1,128]{3,2,1,0:T(1,128)} %param.13) | copy-start | bytes 1179652
  508.5 11.4 %copy-start.5 = (f32[6,256,1,128]{3,1,0,2:T(8,128)}, f32[6,256,1,128]{3,1,0,2:T(8,128)S(1)}, u32[]{:S(2)}) copy-start(f32[6,256,1,128]{3,1,0,2:T(8,128)S(1)} %convolution_bitcast_fusion) | copy-start | bytes 2359300
  508.6 6.7 %collective-permute-start.2 = (f32[6,1,1,128]{3,1,0,2:T(1,128)S(1)}, f32[6,1,1,128]{3,1,0,2:T(1,128)S(1)}, u32[]{:S(2)}, u32[]{:S(2)}) collective-permute-start(f32[6,1,1,128]{3,1,0,2:T(1,128)S(1)} %slice.4306), channel_id=1, source_target_pairs={{0,32},{32,64},{64,96},{96,128},{128,160},{160,192},{192,224},{224... | collective-permute-start | bytes 9224 | tf_op jit(solution)/shard_map/ppermute | solution.py:19
  515.9 52.1 %collective-permute-start.3 = (f32[6,1,1,128]{3,1,0,2:T(1,128)}, f32[6,1,1,128]{3,1,0,2:T(1,128)}, u32[]{:S(2)}, u32[]{:S(2)}) collective-permute-start(f32[6,1,1,128]{3,1,0,2:T(1,128)} %get-tuple-element.1124), channel_id=1, source_target_pairs={{32,0},{64,32},{96,64},{128,96},{160,128},{192,160},{224,192},{256... | collective-permute-start | bytes 9224 | tf_op jit(solution)/shard_map/ppermute | solution.py:22
  532.9 4.0 copy-start.16
  532.9 4.0 copy-start.17
  539.0 29.0 %copy-start.6 = (f32[6,256,1,128]{3,1,0,2:T(8,128)S(1)}, f32[6,256,1,128]{3,1,0,2:T(8,128)}, u32[]{:S(2)}) copy-start(f32[6,256,1,128]{3,1,0,2:T(8,128)} %copy-done.5) | copy-start | bytes 2359300
  539.4 37.4 %copy-start.2 = (f32[1,256,1,128]{3,2,1,0:T(1,128)S(1)}, f32[1,256,1,128]{3,2,1,0:T(1,128)}, u32[]{:S(2)}) copy-start(f32[1,256,1,128]{3,2,1,0:T(1,128)} %copy-done.1) | copy-start | bytes 393220
  541.1 41.6 %copy-start.8 = (f32[1,256]{1,0:T(1,128)S(1)}, f32[1,256]{1,0:T(1,128)}, u32[]{:S(2)}) copy-start(f32[1,256]{1,0:T(1,128)} %get-tuple-element.1199) | copy-start | bytes 3076
  541.1 41.6 %copy-start.9 = (f32[1,256]{1,0:T(1,128)S(1)}, f32[1,256]{1,0:T(1,128)}, u32[]{:S(2)}) copy-start(f32[1,256]{1,0:T(1,128)} %get-tuple-element.1200) | copy-start | bytes 3076
  541.1 41.6 %copy-start.10 = (f32[1,256]{1,0:T(1,128)S(1)}, f32[1,256]{1,0:T(1,128)}, u32[]{:S(2)}) copy-start(f32[1,256]{1,0:T(1,128)} %get-tuple-element.1201) | copy-start | bytes 3076
  541.1 41.6 %copy-start.11 = (f32[1,256]{1,0:T(1,128)S(1)}, f32[1,256]{1,0:T(1,128)}, u32[]{:S(2)}) copy-start(f32[1,256]{1,0:T(1,128)} %get-tuple-element.1202) | copy-start | bytes 3076
  541.1 41.6 %copy-start.12 = (f32[1,256]{1,0:T(1,128)S(1)}, f32[1,256]{1,0:T(1,128)}, u32[]{:S(2)}) copy-start(f32[1,256]{1,0:T(1,128)} %get-tuple-element.1203) | copy-start | bytes 3076
  541.1 41.6 %copy-start.13 = (f32[1,256]{1,0:T(1,128)S(1)}, f32[1,256]{1,0:T(1,128)}, u32[]{:S(2)}) copy-start(f32[1,256]{1,0:T(1,128)} %get-tuple-element.1204) | copy-start | bytes 3076
  541.2 41.6 %copy-start.14 = (f32[1,256]{1,0:T(1,128)S(1)}, f32[1,256]{1,0:T(1,128)}, u32[]{:S(2)}) copy-start(f32[1,256]{1,0:T(1,128)} %get-tuple-element.1205) | copy-start | bytes 3076
  541.2 41.6 %copy-start.15 = (f32[1,256]{1,0:T(1,128)S(1)}, f32[1,256]{1,0:T(1,128)}, u32[]{:S(2)}) copy-start(f32[1,256]{1,0:T(1,128)} %get-tuple-element.1206) | copy-start | bytes 3076
  541.2 62.0 %copy-start.4 = (f32[7,32,256]{2,1,0:T(8,128)S(1)}, f32[7,32,256]{2,1,0:T(8,128)}, u32[]{:S(2)}) copy-start(f32[7,32,256]{2,1,0:T(8,128)} %copy-done.3) | copy-start | bytes 688132
  560.6 16.2 %all-to-all-start.1 = ((f32[32,3,8,1,128]{4,2,1,3,0:T(8,128)}), f32[32,3,8,1,128]{4,2,1,3,0:T(8,128)S(1)}, u32[]{:S(2)}, u32[]{:S(2)}) async-start(f32[32,3,8,1,128]{4,2,1,3,0:T(8,128)} %constant_dynamic-update-slice_fusion), calls=%async_computation.1 | async-start | bytes 786432 | tf_op jit(solution)/shard_map/all_to_all | solution.py:153
  576.9 26.4 %collective-permute-start.4 = (f32[3,3,1,128]{3,1,0,2:T(4,128)S(1)}, f32[3,3,1,128]{3,1,0,2:T(4,128)S(1)}, u32[]{:S(2)}, u32[]{:S(2)}) collective-permute-start(f32[3,3,1,128]{3,1,0,2:T(4,128)S(1)} %get-tuple-element.1133), channel_id=1, source_target_pairs={{32,0},{64,32},{96,64},{128,96},{160,128},{192,160},{224,192},{256... | collective-permute-start | bytes 13832 | tf_op jit(solution)/shard_map/ppermute | solution.py:22
  580.5 22.8 %collective-permute-start.5 = (f32[3,3,1,128]{3,1,0,2:T(4,128)S(1)}, f32[3,3,1,128]{3,1,0,2:T(4,128)S(1)}, u32[]{:S(2)}, u32[]{:S(2)}) collective-permute-start(f32[3,3,1,128]{3,1,0,2:T(4,128)S(1)} %get-tuple-element.1134), channel_id=1, source_target_pairs={{0,32},{32,64},{64,96},{96,128},{128,160},{160,192},{192,224},{224... | collective-permute-start | bytes 13832 | tf_op jit(solution)/shard_map/ppermute | solution.py:19
  604.2 6.7 %collective-permute-start.6 = (f32[3,1,1,128]{3,1,0,2:T(1,128)S(1)}, f32[3,1,1,128]{3,1,0,2:T(1,128)S(1)}, u32[]{:S(2)}, u32[]{:S(2)}) collective-permute-start(f32[3,1,1,128]{3,1,0,2:T(1,128)S(1)} %slice.4403), channel_id=1, source_target_pairs={{0,32},{32,64},{64,96},{96,128},{128,160},{160,192},{192,224},{224... | collective-permute-start | bytes 4616 | tf_op jit(solution)/shard_map/ppermute | solution.py:19
  610.9 5.5 collective-permute-start.7
